TPU v7x, 256 devices: a whole 4x4x8 slice. The times are simulated.
256 devices in a mesh: prow: 32 (over x, y, core), pcol: 8 (over z).
Axes of the slice: x: 4, y: 4, z: 8, core: 2. Of those that a mesh axis runs over, the one named last changes fastest.
Arguments:
- right_zero: bfloat16 [32, 8, 1, 512, 512], P('prow', 'pcol'), may hold values from -6 to 6
- inverse_zero: bfloat16 [32, 8, 1, 512, 512], P('prow', 'pcol'), as said below
- factor_blocks: bfloat16 [32, 8, 6, 512, 512], P('prow', 'pcol'), may hold values from -0.046875 to 0.046875
- block_rows: int32 [32, 8, 6], P('prow', 'pcol'), may hold values from 0 to 3, as said below
- block_cols: int32 [32, 8, 6], P('prow', 'pcol'), may hold values from 0 to 7
- block_count: int32 [32, 8], P('prow', 'pcol'), may hold values from 1 to 6, as said below
- right_one: bfloat16 [8, 4, 512, 512], P('pcol'), may hold values from -6 to 6
- inverse_one: bfloat16 [8, 4, 512, 512], P('pcol'), as said below
Outputs:
- solved_zero: bfloat16 [32, 8, 1, 512, 512], P('prow', 'pcol')
- solved_one: bfloat16 [8, 4, 512, 512], P('pcol')
Inputs may be any that keep to these rules, and one draw needn't show every extreme that they name: `block_count`: some grid position uses exactly 6 blocks. Among the first block_count entries of a grid position, the pairs (block_rows, block_cols) are distinct. `inverse_zero`: each [512, 512] matrix is lower triangular with a positive diagonal. `inverse_one`: each [512, 512] matrix is lower triangular with a positive diagonal.
All inputs are finite; a program needn't handle non-finite values.
Results may differ from a plain program's by a relative error of at most 0.0053.
Values may be sent and summed in bfloat16 or wider, within the bound.
A program may use at most 64 MiB of HBM per device.

v0:
```python
import jax
import jax.numpy as jnp
from jax import lax
from jax.sharding import PartitionSpec as P


def body(
    right_zero,
    inverse_zero,
    factor_blocks,
    block_rows,
    block_cols,
    block_count,
    right_one,
    inverse_one,
):
    solved = jnp.einsum(
        "kij,kjn->kin", inverse_zero[0, 0], right_zero[0, 0], preferred_element_type=jnp.float32
    ).astype(jnp.bfloat16)
    solved_zero = solved[None, None]
    per_device = right_zero.shape[2]
    blocks = factor_blocks[0, 0]
    row_list = block_rows[0, 0]
    col_list = block_cols[0, 0]
    block_total = block_count[0, 0]
    groups = right_one.shape[1]
    block_width = right_one.shape[2]
    columns_all = right_one.shape[3]
    zero_update = jnp.zeros((groups, block_width, columns_all), jnp.float32)
    panel_piece = lax.all_gather(solved_zero, "pcol", axis=1, tiled=True)
    held_panels = panel_piece.shape[1] * per_device
    panels = panel_piece.reshape(held_panels, panel_piece.shape[3], panel_piece.shape[4])

    def one_block(b, carry_sum):
        local_col = col_list[b]
        inside = jnp.logical_and(local_col >= 0, local_col < held_panels)

        def add_block(current):
            chosen_panel = lax.dynamic_index_in_dim(
                panels, jnp.clip(local_col, 0, held_panels - 1), 0, keepdims=False
            )
            factor = lax.dynamic_index_in_dim(blocks, b, 0, keepdims=False)
            product = jnp.dot(factor, chosen_panel, preferred_element_type=jnp.float32)
            target = row_list[b]
            before = lax.dynamic_index_in_dim(current, target, 0, keepdims=False)
            return lax.dynamic_update_index_in_dim(current, before + product, target, 0)

        return lax.cond(inside, add_block, lambda current: current, carry_sum)

    update = lax.fori_loop(0, block_total, one_block, zero_update)
    summed = lax.psum(update, "prow")
    residual = (right_one[0].astype(jnp.float32) - summed).astype(jnp.bfloat16)
    solved_one = jnp.einsum(
        "mij,mjn->min", inverse_one[0], residual, preferred_element_type=jnp.float32
    ).astype(jnp.bfloat16)[None]
    return (solved_zero, solved_one)


def solution(mesh):
    in_specs = (
        P("prow", "pcol", None, None, None),
        P("prow", "pcol", None, None, None),
        P("prow", "pcol", None, None, None),
        P("prow", "pcol", None),
        P("prow", "pcol", None),
        P("prow", "pcol"),
        P("pcol", None, None, None),
        P("pcol", None, None, None),
    )
    out_specs = (P("prow", "pcol", None, None, None), P("pcol", None, None, None))
    return jax.shard_map(body, mesh=mesh, in_specs=in_specs, out_specs=out_specs, check_vma=False)
```

profile of v0, /device:TPU:1, one launch (start us, length us, event | category | flops | bytes accessed | tf_op | source)
XLA Modules:
  0.0 263.9 jit_solution(2267609545361282940)
XLA Ops:
  7.2 0.0 copy-start
  7.2 0.0 copy-start.1
  7.2 0.0 copy-start.2
  7.2 0.0 all-gather.3.cloned.1.call-start
  7.2 2.6 convolution_convert_fusion
  9.8 0.0 all-gather.3.cloned.1.call-update
  9.8 0.0 all-reduce.2.cloned.1.call-start
  9.9 59.2 %all-gather.3.cloned.1.call-done = bf16[4096,512]{1,0:T(8,128)(2,1)} async-done(((bf16[512,512]{1,0:T(8,128)(2,1)}), bf16[4096,512]{1,0:T(8,128)(2,1)}) %all-gather.3.cloned.1.call-update) | async-done | bytes 4194320 | tf_op jit(solution)/shard_map/all_gather | solution.py:30
  69.0 2.5 broadcast_in_dim.14
  71.6 0.0 copy-done.1
  71.6 0.0 copy-done.2
  71.6 10.3 %while.13 = (s32[]{:T(128)}, f32[4,512,512]{2,1,0:T(8,128)}, s32[]{:T(128)}, s32[6]{0:T(128)S(1)}, s32[6]{0:T(128)S(1)}, /*index=5*/bf16[6,512,512]{2,1,0:T(8,12...) while((s32[]{:T(128)}, f32[4,512,512]{2,1,0:T(8,128)}, ...), condition=%wide.region_3.4_spmd, body=%wide.region_0.3_spmd.sunk | while | flops 268697600 | bytes 5243237 | solution.py:50
  72.2 0.7 dynamic_slice.28
  74.3 7.0 %conditional.2 = (f32[4,512,512]{2,1,0:T(8,128)}) conditional(s32[]{:T(128)} %convert_element_type.36, f32[4,512,512]{2,1,0:T(8,128)} %get-tuple-element.135, (s32[]{:T(128)}, s32[6]{0:T(128)S(1)}, f32[4,512,512]{2,1,0:T(8,128)}, bf16[6,512,512]{2,1,0:T(8,128)(2,1)}, s32[]{:T(128)}, /*index=5*/bf16[8,512,512]{2,1,0:T(8,128)(2,1)}) %tuple.30), branch_computations={%region_1.0_spmd, %region_2.2_spmd} | conditional | flops 268697600 | bytes 5243008 | solution.py:48
  74.3 0.6 dynamic_slice.13
  76.6 1.3 constant_dynamic-slice_fusion
  78.6 2.7 %fusion.1 = f32[4,512,512]{2,1,0:T(8,128)} fusion(f32[4,512,512]{2,1,0:T(8,128)} %get-tuple-element.44, s32[]{:T(128)S(6)} %select_n.14, f32[1,512,512]{2,1,0:T(8,128)S(1)} %constant_dynamic-slice_fusion, bf16[8,512,512]{2,1,0:T(8,128)(2,1)} %get-tuple-element.48, s32[]{:T(128)S(6)} %min.3, bf16[6,512,512]{2,1,0:T(8,128)(2,1)} %get-tuple-element.47, ...), kind=kOutput, calls=%fused_computation.2 | convolution fusion | flops 268697600 | bytes 3145740 | tf_op jit(solution)/shard_map/while/body/cond/branch_1_fun/dot_general | solution.py:43
  81.9 0.0 all-reduce.2.cloned.1.call-update
  81.9 165.4 %all-reduce.2.cloned.1.call-done = f32[4,512,512]{2,1,0:T(8,128)} async-done(((f32[4,512,512]{2,1,0:T(8,128)}), f32[4,512,512]{2,1,0:T(8,128)}) %all-reduce.2.cloned.1.call-update) | async-done | bytes 4194320 | tf_op jit(solution)/shard_map/psum | solution.py:51
  247.3 0.0 copy-done
  247.3 5.6 %convert_bitcast_fusion = bf16[1,4,512,512]{2,3,1,0:T(8,128)(2,1)} fusion(bf16[1,4,512,512]{3,2,1,0:T(8,128)(2,1)S(1)} %copy-done, f32[4,512,512]{2,1,0:T(8,128)} %all-reduce.2.cloned.1.call-done, bf16[1,4,512,512]{3,2,1,0:T(8,128)(2,1)} %param.18), kind=kOutput, calls=%fused_computation.14 | convolution fusion | flops 1077936128 | bytes 10485760 | tf_op jit(solution)/shard_map/mij,mjn->min/dot_general | solution.py:53
  252.9 4.1 %copy.11 = bf16[1,4,512,512]{3,2,1,0:T(8,128)(2,1)} copy(bf16[1,4,512,512]{2,3,1,0:T(8,128)(2,1)} %convert_bitcast_fusion) | data formatting | bytes 4194304
Async XLA Ops:
  7.2 240.1 %copy-start = (bf16[1,4,512,512]{3,2,1,0:T(8,128)(2,1)S(1)}, bf16[1,4,512,512]{3,2,1,0:T(8,128)(2,1)}, u32[]{:S(2)}) copy-start(bf16[1,4,512,512]{3,2,1,0:T(8,128)(2,1)} %param.19) | copy-start | bytes 6291460
  7.2 64.4 %copy-start.1 = (s32[1,1,6]{2,1,0:T(1,128)S(1)}, s32[1,1,6]{2,1,0:T(1,128)}, u32[]{:S(2)}) copy-start(s32[1,1,6]{2,1,0:T(1,128)} %param.16) | copy-start | bytes 76
  7.2 64.4 %copy-start.2 = (s32[1,1,6]{2,1,0:T(1,128)S(1)}, s32[1,1,6]{2,1,0:T(1,128)}, u32[]{:S(2)}) copy-start(s32[1,1,6]{2,1,0:T(1,128)} %param.15) | copy-start | bytes 76
  7.2 61.9 %all-gather.3.cloned.1.call-start = ((), (), s32[]{:S(2)}) async-start(), calls=%async_computation.1 | async-start | bytes 4718592 | tf_op jit(solution)/shard_map/all_gather | solution.py:30
  9.8 237.5 %all-reduce.2.cloned.1.call-start = ((), (), s32[]{:S(2)}) async-start(), calls=%async_computation | async-start | bytes 8388608 | tf_op jit(solution)/shard_map/psum | solution.py:51
Sparse Core Ops, SparseCore 0:
  10.4 58.6 all-gather.2
  82.0 165.2 all-reduce.1
where the time goes:
time: 264 us
  waiting for transfers between devices  225 us (85%)
  between operations  14.1 us (5%)
  matrix products  10.9 us (4%)
  local copies, waits for them, and re-layouts  9.2 us (3%)
  loops' own time  5.11 us (2%)
    psum x1, waiting for transfers between devices, body(): summed = lax.psum(update, 'prow')  165 us
    all_gather x1, waiting for transfers between devices, body(): panel_piece = lax.all_gather(solved_zero, 'pcol', axis=1, tiled=True)  59.2 us
    dot_general x1, matrix products, body(): jnp.einsum('mij,mjn->min', inverse_one[0], residual, preferred_element_ty...  5.65 us
  transfers between devices with their start and end apart: 2, of which 2 were waited for; matrix products, arithmetic and copies ran while one was open for 0% of the time, Pallas kernels for 0%

commit v1 on v0

v1 whole, which is shorter than its diff:
```python
import functools

import jax
import jax.numpy as jnp
from jax import lax
from jax.experimental import pallas as pl
from jax.experimental.pallas import tpu as pltpu
from jax.sharding import PartitionSpec as P

MESH = pl.DeviceIdType.MESH
BF = jnp.bfloat16
F32 = jnp.float32
W = 512
CW = 128
NCH = 4
NZ = 8
CHIPS = 16
OWN = 64
HALF = 1024


def fused(
    rows_s, cols_s, count_s, inv_hbm, right_hbm, blocks_hbm, right_one_hbm,
    res_out, own_out,
    inv_v, right_v, blocks_v, ro_v, acc,
    p0, p1, p2, p3,
    pair_send, pair_recv, rs_send, rs_recv, res_v,
    load_sem, out_sem, z_send, z_recv, pair_ssem, pair_rsem, rs_ssem, rs_rsem, ag_ssem, ag_rsem,
    sib_ssem, sib_rsem,
):
    panels = (p0, p1, p2, p3)
    r = lax.axis_index("prow")
    z = lax.axis_index("pcol")
    core = lax.rem(r, 2)
    chip = r // 2
    up = lax.rem(z + 1, NZ)
    down = lax.rem(z + NZ - 1, NZ)
    sibling = chip * 2 + 1 - core

    def peer(j):
        return lax.rem(chip + j, CHIPS) * 2 + core

    cp_inv = pltpu.make_async_copy(inv_hbm, inv_v, load_sem.at[0])
    cp_right = pltpu.make_async_copy(right_hbm, right_v, load_sem.at[1])
    cp_inv.start()
    cp_right.start()

    barrier = pltpu.get_barrier_semaphore()
    for zz in (up, down):
        pl.semaphore_signal(barrier, inc=1, device_id=(r, zz), device_id_type=MESH)
    pl.semaphore_signal(barrier, inc=1, device_id=(sibling, z), device_id_type=MESH)

    def greet(j, carry):
        pl.semaphore_signal(barrier, inc=1, device_id=(peer(j), z), device_id_type=MESH)
        return carry

    lax.fori_loop(1, CHIPS, greet, 0)

    cp_blocks = pltpu.make_async_copy(blocks_hbm, blocks_v, load_sem.at[2])
    cp_blocks.start()
    my_rows = pl.multiple_of(lax.rem(chip, 8) * OWN, OWN)
    cp_ro = pltpu.make_async_copy(
        right_one_hbm.at[core * 2 + chip // 8, pl.ds(my_rows, OWN), :], ro_v, load_sem.at[3]
    )
    cp_ro.start()

    def own_panel(k):
        panels[k][z] = jnp.dot(
            inv_v[...], right_v[:, k * CW:(k + 1) * CW], preferred_element_type=F32
        ).astype(BF)

    def z_copy(k, way, half, d):
        origin = lax.rem(z - d + NZ, NZ) if way == 0 else lax.rem(z + d, NZ)
        piece = panels[k].at[origin, pl.ds(half * 256, 256), :]
        return pltpu.make_async_remote_copy(
            src_ref=piece,
            dst_ref=piece,
            send_sem=z_send.at[k],
            recv_sem=z_recv.at[k, way, half, d],
            device_id=(r, up if way == 0 else down),
            device_id_type=MESH,
        )

    def z_arrive(k, way, half, d):
        origin = lax.rem(z - d - 1 + NZ, NZ) if way == 0 else lax.rem(z + d + 1, NZ)
        piece = panels[k].at[origin, pl.ds(half * 256, 256), :]
        pltpu.make_async_copy(piece, piece, z_recv.at[k, way, half, d]).wait()

    def z_step(k, d):
        order = ((0, 0), (1, 1), (0, 1), (1, 0)) if d < 3 else ((0, 0), (1, 1))
        for way, half in order:
            if d > 0:
                z_arrive(k, way, half, d - 1)
            z_copy(k, way, half, d).start()

    def z_final(k):
        z_arrive(k, 0, 1, 2)
        z_arrive(k, 1, 0, 2)
        z_arrive(k, 0, 0, 3)
        z_arrive(k, 1, 1, 3)

    def pair_copy(k):
        return pltpu.make_async_remote_copy(
            src_ref=pair_send.at[k], dst_ref=pair_recv.at[k],
            send_sem=pair_ssem.at[k], recv_sem=pair_rsem.at[k],
            device_id=(sibling, z), device_id_type=MESH,
        )

    def stage_a(k):
        acc[...] = jnp.zeros_like(acc)

        def block(b, carry):
            product = jnp.dot(blocks_v[b], panels[k][cols_s[b]], preferred_element_type=F32)
            used = b < count_s[0]
            for m in range(4):
                weight = jnp.where(jnp.logical_and(used, rows_s[b] == m), 1.0, 0.0)
                acc[m] += product * weight
            return carry

        lax.fori_loop(0, 6, block, 0)
        away = 2 - core * 2
        for i in range(2):
            pair_send[k, i * W:(i + 1) * W, :] = acc[away + i].astype(BF)
        pair_copy(k).start()

    def rs_copy(k, j):
        target = lax.rem(chip + j, CHIPS)
        return pltpu.make_async_remote_copy(
            src_ref=rs_send.at[k, pl.ds(pl.multiple_of(target * OWN, OWN), OWN), :],
            dst_ref=rs_recv.at[k, j - 1],
            send_sem=rs_ssem.at[k], recv_sem=rs_rsem.at[k],
            device_id=(peer(j), z), device_id_type=MESH,
        )

    def stage_b(k):
        pair_copy(k).wait()
        for i in range(2):
            both = acc[core * 2 + i] + pair_recv[k, i * W:(i + 1) * W, :].astype(F32)
            rs_send[k, i * W:(i + 1) * W, :] = both.astype(BF)

        def send(j, carry):
            rs_copy(k, j).start()
            return carry

        lax.fori_loop(1, CHIPS, send, 0)

    def own_rows():
        return pl.ds(pl.multiple_of(core * HALF + chip * OWN, OWN), OWN)

    def ag_copy(k, j):
        piece = res_v.at[k, own_rows(), :]
        return pltpu.make_async_remote_copy(
            src_ref=piece, dst_ref=piece,
            send_sem=ag_ssem.at[k], recv_sem=ag_rsem.at[k],
            device_id=(peer(j), z), device_id_type=MESH,
        )

    def all_bytes(k, sem):
        return pltpu.make_async_copy(rs_recv.at[k], rs_recv.at[k], sem.at[k])

    def stage_c(k):
        all_bytes(k, rs_rsem).wait()
        total = rs_send[k, pl.ds(pl.multiple_of(chip * OWN, OWN), OWN), :].astype(F32)
        for j in range(CHIPS - 1):
            total += rs_recv[k, j].astype(F32)
        left = ro_v[:, k * CW:(k + 1) * CW].astype(F32) - total
        res_v[k, own_rows(), :] = left.astype(BF)

        def send(j, carry):
            ag_copy(k, j).start()
            return carry

        lax.fori_loop(1, CHIPS, send, 0)

    def sib_copy(k):
        piece = res_v.at[k, pl.ds(pl.multiple_of(core * HALF, HALF), HALF), :]
        return pltpu.make_async_remote_copy(
            src_ref=piece, dst_ref=piece,
            send_sem=sib_ssem.at[k], recv_sem=sib_rsem.at[k],
            device_id=(sibling, z), device_id_type=MESH,
        )

    def stage_d(k):
        all_bytes(k, ag_rsem).wait()
        sib_copy(k).start()

    def out_copy(k):
        return pltpu.make_async_copy(res_v.at[k], res_out.at[k], out_sem.at[k])

    def own_copy(k):
        return pltpu.make_async_copy(panels[k].at[z], own_out.at[k], out_sem.at[NCH + k])

    def stage_e(k):
        sib_copy(k).wait()
        out_copy(k).start()

    cp_inv.wait()
    cp_right.wait()
    own_panel(0)
    pl.semaphore_wait(barrier, CHIPS + 2)
    z_step(0, 0)
    for k in range(1, NCH):
        own_panel(k)
    cp_blocks.wait()
    cp_ro.wait()
    for k in range(NCH):
        own_copy(k).start()

    z_step(0, 1)
    z_step(0, 2)
    z_step(1, 0)
    z_step(0, 3)
    z_final(0)

    z_step(1, 1)
    stage_a(0)
    z_step(1, 2)
    stage_b(0)
    z_step(2, 0)
    z_step(1, 3)
    z_final(1)

    z_step(2, 1)
    stage_a(1)
    stage_c(0)
    z_step(2, 2)
    stage_b(1)
    stage_d(0)
    z_step(3, 0)
    z_step(2, 3)
    z_final(2)

    z_step(3, 1)
    stage_e(0)
    stage_a(2)
    stage_c(1)
    z_step(3, 2)
    stage_b(2)
    stage_d(1)
    z_step(3, 3)
    stage_c(2)
    z_final(3)

    stage_e(1)
    stage_a(3)
    stage_b(3)
    stage_d(2)
    stage_c(3)
    stage_e(2)
    stage_d(3)
    stage_e(3)

    for k in range(NCH):
        piece = panels[k].at[0:7]
        pltpu.make_async_copy(piece, piece, z_send.at[k]).wait()
        all_bytes(k, rs_ssem).wait()
        all_bytes(k, ag_ssem).wait()
        out_copy(k).wait()
        own_copy(k).wait()


def finish(inv_ref, res_ref, own_ref, one_ref, zero_ref):
    for c in range(NCH):
        one_ref[0, :, c * CW:(c + 1) * CW] = jnp.dot(
            inv_ref[0], res_ref[c], preferred_element_type=F32
        ).astype(BF)
    zero_ref[...] = own_ref[0]


def body(
    right_zero, inverse_zero, factor_blocks, block_rows, block_cols, block_count, right_one, inverse_one,
):
    smem = pl.BlockSpec(memory_space=pltpu.SMEM)
    hbm = pl.BlockSpec(memory_space=pl.ANY)
    dma = pltpu.SemaphoreType.DMA
    res, own = pl.pallas_call(
        fused,
        out_shape=(
            jax.ShapeDtypeStruct((NCH, 4 * W, CW), BF),
            jax.ShapeDtypeStruct((NCH, W, CW), BF),
        ),
        in_specs=[smem, smem, smem, hbm, hbm, hbm, hbm],
        out_specs=(hbm, hbm),
        scratch_shapes=[
            pltpu.VMEM((W, W), BF),
            pltpu.VMEM((W, W), BF),
            pltpu.VMEM((6, W, W), BF),
            pltpu.VMEM((OWN, W), BF),
            pltpu.VMEM((4, W, CW), F32),
        ]
        + [pltpu.VMEM((NZ, W, CW), BF)] * NCH
        + [
            pltpu.VMEM((NCH, HALF, CW), BF),
            pltpu.VMEM((NCH, HALF, CW), BF),
            pltpu.VMEM((NCH, HALF, CW), BF),
            pltpu.VMEM((NCH, CHIPS - 1, OWN, CW), BF),
            pltpu.VMEM((NCH, 4 * W, CW), BF),
            dma((4,)),
            dma((2 * NCH,)),
            dma((NCH,)),
            dma((NCH, 2, 2, 4)),
            dma((NCH,)), dma((NCH,)),
            dma((NCH,)), dma((NCH,)),
            dma((NCH,)), dma((NCH,)),
            dma((NCH,)), dma((NCH,)),
        ],
        compiler_params=pltpu.CompilerParams(
            collective_id=0, has_side_effects=True, vmem_limit_bytes=40 * 1024 * 1024
        ),
    )(
        block_rows[0, 0], block_cols[0, 0], block_count[0],
        inverse_zero[0, 0, 0], right_zero[0, 0, 0], factor_blocks[0, 0], right_one[0],
    )
    one, zero = pl.pallas_call(
        finish,
        grid=(4,),
        out_shape=(
            jax.ShapeDtypeStruct((4, W, W), BF),
            jax.ShapeDtypeStruct((W, W), BF),
        ),
        in_specs=[
            pl.BlockSpec((1, W, W), lambda m: (m, 0, 0)),
            pl.BlockSpec((NCH, W, CW), lambda m: (0, m, 0)),
            pl.BlockSpec((1, W, CW), lambda m: (m, 0, 0)),
        ],
        out_specs=(
            pl.BlockSpec((1, W, W), lambda m: (m, 0, 0)),
            pl.BlockSpec((W, CW), lambda m: (0, m)),
        ),
    )(inverse_one[0], res, own)
    return (zero[None, None, None], one[None])


def solution(mesh):
    in_specs = (
        P("prow", "pcol", None, None, None),
        P("prow", "pcol", None, None, None),
        P("prow", "pcol", None, None, None),
        P("prow", "pcol", None),
        P("prow", "pcol", None),
        P("prow", "pcol"),
        P("pcol", None, None, None),
        P("pcol", None, None, None),
    )
    out_specs = (P("prow", "pcol", None, None, None), P("pcol", None, None, None))
    return jax.shard_map(body, mesh=mesh, in_specs=in_specs, out_specs=out_specs, check_vma=False)
```

time: 264 us -> 102 us (0.39)
  waiting for transfers between devices: 225 us -> 0 us
  Pallas kernels: 0 us -> 91 us
  between operations: 14.1 us -> 1.31 us
  matrix products: 10.9 us -> 0 us
  loops' own time: 5.11 us -> 0 us
    psum x1 -> x0, waiting for transfers between devices: 165 us -> none  [body(): summed = lax.psum(update, 'prow')]
    pallas_call x0 -> x2, Pallas kernels: none -> 91 us  [the longest x1 85.3 us: body(): pl.pallas_call(fused, out_shape=(jax.ShapeDtypeStruct((NCH, 4 * W, CW), B...]
    all_gather x1 -> x0, waiting for transfers between devices: 59.2 us -> none  [body(): panel_piece = lax.all_gather(solved_zero, 'pcol', axis=1, tiled=True)]
    dot_general x3 -> x0, matrix products: 10.9 us -> none  [the longest x1 5.65 us: body(): jnp.einsum('mij,mjn->min', inverse_one[0], residual, preferred_element_ty...]
    another operation x2 -> x0, loops' own time: 5.11 us -> none  [the longest x1 2.69 us: body(): update = lax.fori_loop(0, block_total, one_block, zero_update)]
    unnamed x7 -> x16, local copies, waits for them, and re-layouts: 4.15 us -> 9 us
  transfers between devices with their start and end apart: 2 -> 0, of which waited for: 2 -> 0; matrix products, arithmetic and copies ran while one was open for 0% -> 0% of each run, Pallas kernels for 0% -> 0%
where the time goes in v1:
time: 102 us; the launch traced here: 101 us
  Pallas kernels  91 us (89%)
  local copies, waits for them, and re-layouts  9 us (9%)
  between operations  1.31 us (1%)
    pallas_call x1, Pallas kernels, body(): pl.pallas_call(fused, out_shape=(jax.ShapeDtypeStruct((NCH, 4 * W, CW), B...  85.3 us
    unnamed x16, local copies, waits for them, and re-layouts  9 us
    pallas_call x1, Pallas kernels, body(): pl.pallas_call(finish, grid=(4,), out_shape=(jax.ShapeDtypeStruct((4, W,...  5.69 us

profile of v1, /device:TPU:1, one launch (start us, length us, event | category | flops | bytes accessed | tf_op | source)
XLA Modules:
  0.0 101.3 jit_solution(16596450365956929528)
XLA Ops:
  1.3 0.0 copy-start
  1.3 1.9 %copy-done = bf16[1,1,6,512,512]{4,3,2,1,0:T(8,128)(2,1)S(1)} copy-done((bf16[1,1,6,512,512]{4,3,2,1,0:T(8,128)(2,1)S(1)}, bf16[1,1,6,512,512]{4,3,2,1,0:T(8,128)(2,1)}, u32[]{:S(2)}) %copy-start) | copy-done | bytes 3145752
  3.2 0.0 copy-start.1
  3.2 1.6 %copy-done.1 = bf16[1,4,512,512]{3,2,1,0:T(8,128)(2,1)S(1)} copy-done((bf16[1,4,512,512]{3,2,1,0:T(8,128)(2,1)S(1)}, bf16[1,4,512,512]{3,2,1,0:T(8,128)(2,1)}, u32[]{:S(2)}) %copy-start.1) | copy-done | bytes 2097176
  4.8 0.0 copy-start.4
  4.8 1.0 %copy-done.4 = bf16[1,1,1,512,512]{4,3,2,1,0:T(8,128)(2,1)S(1)} copy-done((bf16[1,1,1,512,512]{4,3,2,1,0:T(8,128)(2,1)S(1)}, bf16[1,1,1,512,512]{4,3,2,1,0:T(8,128)(2,1)}, u32[]{:S(2)}) %copy-start.4) | copy-done | bytes 524312
  5.8 0.0 copy-start.5
  5.8 1.0 %copy-done.5 = bf16[1,1,1,512,512]{4,3,2,1,0:T(8,128)(2,1)S(1)} copy-done((bf16[1,1,1,512,512]{4,3,2,1,0:T(8,128)(2,1)S(1)}, bf16[1,1,1,512,512]{4,3,2,1,0:T(8,128)(2,1)}, u32[]{:S(2)}) %copy-start.5) | copy-done | bytes 524312
  6.8 0.0 copy-start.6
  6.8 0.7 copy-done.6
  7.5 0.0 copy-start.7
  7.5 0.7 copy-done.7
  8.2 85.3 %shard_map.95 = (bf16[4,2048,128]{2,1,0:T(8,128)(2,1)S(1)}, bf16[4,512,128]{2,1,0:T(8,128)(2,1)S(1)}) custom-call(s32[6]{0:T(128)S(1)} %bitcast.15, s32[6]{0:T(128)S(1)} %bitcast.16, s32[1]{0:T(128)} %bitcast.10.count_s, bf16[512,512]{1,0:T(8,128)(2,1)S(1)} %bitcast.13, bf16[512,512]{1,0:T(8,128)(2,1)S(1)} %bitcast.14, bf16[6,512,512]{2,1,0:T(8,128)(2,1)S(1)} %bitcast.11, ...), custom_call_target="tpu_custom_call" | custom-call | tf_op jit(solution)/shard_map/pallas_call | solution.py:276
  93.4 0.0 copy-start.2
  93.4 1.3 %copy-done.2 = bf16[4,2048,128]{2,1,0:T(8,128)(2,1)} copy-done((bf16[4,2048,128]{2,1,0:T(8,128)(2,1)}, bf16[4,2048,128]{2,1,0:T(8,128)(2,1)S(1)}, u32[]{:S(2)}) %copy-start.2) | copy-done | bytes 2097176
  94.8 0.0 copy-start.3
  94.8 0.8 copy-done.3
  95.6 5.7 %shard_map.96 = (bf16[4,512,512]{2,1,0:T(8,128)(2,1)}, bf16[512,512]{1,0:T(8,128)(2,1)}) custom-call(bf16[4,512,512]{2,1,0:T(8,128)(2,1)} %bitcast.17, bf16[4,2048,128]{2,1,0:T(8,128)(2,1)} %copy-done.2, bf16[4,512,128]{2,1,0:T(8,128)(2,1)} %copy-done.3), custom_call_target="tpu_custom_call" | custom-call | tf_op jit(solution)/shard_map/pallas_call | solution.py:314
Async XLA Ops:
  1.3 1.9 %copy-start = (bf16[1,1,6,512,512]{4,3,2,1,0:T(8,128)(2,1)S(1)}, bf16[1,1,6,512,512]{4,3,2,1,0:T(8,128)(2,1)}, u32[]{:S(2)}) copy-start(bf16[1,1,6,512,512]{4,3,2,1,0:T(8,128)(2,1)} %param.10) | copy-start | bytes 9437188
  3.2 1.6 %copy-start.1 = (bf16[1,4,512,512]{3,2,1,0:T(8,128)(2,1)S(1)}, bf16[1,4,512,512]{3,2,1,0:T(8,128)(2,1)}, u32[]{:S(2)}) copy-start(bf16[1,4,512,512]{3,2,1,0:T(8,128)(2,1)} %param.14) | copy-start | bytes 6291460
  4.8 1.0 %copy-start.4 = (bf16[1,1,1,512,512]{4,3,2,1,0:T(8,128)(2,1)S(1)}, bf16[1,1,1,512,512]{4,3,2,1,0:T(8,128)(2,1)}, u32[]{:S(2)}) copy-start(bf16[1,1,1,512,512]{4,3,2,1,0:T(8,128)(2,1)} %param.9) | copy-start | bytes 1572868
  5.8 1.0 %copy-start.5 = (bf16[1,1,1,512,512]{4,3,2,1,0:T(8,128)(2,1)S(1)}, bf16[1,1,1,512,512]{4,3,2,1,0:T(8,128)(2,1)}, u32[]{:S(2)}) copy-start(bf16[1,1,1,512,512]{4,3,2,1,0:T(8,128)(2,1)} %param.8) | copy-start | bytes 1572868
  6.8 0.7 copy-start.6
  7.5 0.7 copy-start.7
  93.4 1.3 %copy-start.2 = (bf16[4,2048,128]{2,1,0:T(8,128)(2,1)}, bf16[4,2048,128]{2,1,0:T(8,128)(2,1)S(1)}, u32[]{:S(2)}) copy-start(bf16[4,2048,128]{2,1,0:T(8,128)(2,1)S(1)} %get-tuple-element.6.res_ref) | copy-start | bytes 6291460
  94.8 0.8 copy-start.3

commit v2 on v1

--- a/solution.py
+++ b/solution.py
@@ -20,9 +20,9 @@
 
 
 def fused(
-    rows_s, cols_s, count_s, inv_hbm, right_hbm, blocks_hbm, right_one_hbm,
-    res_out, own_out,
-    inv_v, right_v, blocks_v, ro_v, acc,
+    rows_s, cols_s, count_s, inv_hbm, right_hbm, blocks_hbm, right_one_hbm, inv_one_hbm,
+    one_out, own_out,
+    inv_v, right_v, blocks_v, ro_v, inv_one_v, one_v, own_v, acc,
     p0, p1, p2, p3,
     pair_send, pair_recv, rs_send, rs_recv, res_v,
     load_sem, out_sem, z_send, z_recv, pair_ssem, pair_rsem, rs_ssem, rs_rsem, ag_ssem, ag_rsem,
@@ -58,20 +58,26 @@
 
     cp_blocks = pltpu.make_async_copy(blocks_hbm, blocks_v, load_sem.at[2])
     cp_blocks.start()
-    my_rows = pl.multiple_of(lax.rem(chip, 8) * OWN, OWN)
+    my_rows = pl.multiple_of(core * 256 + lax.rem(chip, 4) * OWN, OWN)
     cp_ro = pltpu.make_async_copy(
-        right_one_hbm.at[core * 2 + chip // 8, pl.ds(my_rows, OWN), :], ro_v, load_sem.at[3]
+        right_one_hbm.at[chip // 4, pl.ds(my_rows, OWN), :], ro_v, load_sem.at[3]
     )
     cp_ro.start()
+    cp_inv_one = pltpu.make_async_copy(inv_one_hbm, inv_one_v, load_sem.at[4])
+    cp_inv_one.start()
 
     def own_panel(k):
-        panels[k][z] = jnp.dot(
-            inv_v[...], right_v[:, k * CW:(k + 1) * CW], preferred_element_type=F32
-        ).astype(BF)
+        x = right_v[:, k * CW:(k + 1) * CW]
+        top = jnp.dot(inv_v[:256, :256], x[:256], preferred_element_type=F32).astype(BF)
+        low = jnp.dot(inv_v[256:, :], x, preferred_element_type=F32).astype(BF)
+        panels[k][z, :256] = top
+        panels[k][z, 256:] = low
+        own_v[:256, k * CW:(k + 1) * CW] = top
+        own_v[256:, k * CW:(k + 1) * CW] = low
 
     def z_copy(k, way, half, d):
         origin = lax.rem(z - d + NZ, NZ) if way == 0 else lax.rem(z + d, NZ)
-        piece = panels[k].at[origin, pl.ds(half * 256, 256), :]
+        piece = panels[k].at[origin, pl.ds(half * 128, 128), :]
         return pltpu.make_async_remote_copy(
             src_ref=piece,
             dst_ref=piece,
@@ -83,21 +89,24 @@
 
     def z_arrive(k, way, half, d):
         origin = lax.rem(z - d - 1 + NZ, NZ) if way == 0 else lax.rem(z + d + 1, NZ)
-        piece = panels[k].at[origin, pl.ds(half * 256, 256), :]
+        piece = panels[k].at[origin, pl.ds(half * 128, 128), :]
         pltpu.make_async_copy(piece, piece, z_recv.at[k, way, half, d]).wait()
 
     def z_step(k, d):
-        order = ((0, 0), (1, 1), (0, 1), (1, 0)) if d < 3 else ((0, 0), (1, 1))
-        for way, half in order:
-            if d > 0:
-                z_arrive(k, way, half, d - 1)
-            z_copy(k, way, half, d).start()
+        for i in range(4):
+            for way in range(2):
+                part = (i + 2 * way) % 4
+                far = (part < 2) if way == 0 else (part >= 2)
+                if d < 3 or far:
+                    if d > 0:
+                        z_arrive(k, way, part, d - 1)
+                    z_copy(k, way, part, d).start()
 
     def z_final(k):
-        z_arrive(k, 0, 1, 2)
-        z_arrive(k, 1, 0, 2)
-        z_arrive(k, 0, 0, 3)
-        z_arrive(k, 1, 1, 3)
+        for part in range(4):
+            for way in range(2):
+                far = (part < 2) if way == 0 else (part >= 2)
+                z_arrive(k, way, part, 3 if far else 2)
 
     def pair_copy(k):
         return pltpu.make_async_remote_copy(
@@ -106,22 +115,26 @@
             device_id=(sibling, z), device_id_type=MESH,
         )
 
-    def stage_a(k):
-        acc[...] = jnp.zeros_like(acc)
+    def products(k, side):
+        rows = pl.ds(pl.multiple_of(side * 256, 256), 256)
+        acc[side] = jnp.zeros((4, 256, CW), F32)
 
         def block(b, carry):
-            product = jnp.dot(blocks_v[b], panels[k][cols_s[b]], preferred_element_type=F32)
+            product = jnp.dot(blocks_v[b, rows, :], panels[k][cols_s[b]], preferred_element_type=F32)
             used = b < count_s[0]
             for m in range(4):
                 weight = jnp.where(jnp.logical_and(used, rows_s[b] == m), 1.0, 0.0)
-                acc[m] += product * weight
+                acc[side, m] += product * weight
             return carry
 
         lax.fori_loop(0, 6, block, 0)
-        away = 2 - core * 2
-        for i in range(2):
-            pair_send[k, i * W:(i + 1) * W, :] = acc[away + i].astype(BF)
+
+    def stage_a(k):
+        products(k, 1 - core)
+        for m in range(4):
+            pair_send[k, m * 256:(m + 1) * 256, :] = acc[1 - core, m].astype(BF)
         pair_copy(k).start()
+        products(k, core)
 
     def rs_copy(k, j):
         target = lax.rem(chip + j, CHIPS)
@@ -134,9 +147,9 @@
 
     def stage_b(k):
         pair_copy(k).wait()
-        for i in range(2):
-            both = acc[core * 2 + i] + pair_recv[k, i * W:(i + 1) * W, :].astype(F32)
-            rs_send[k, i * W:(i + 1) * W, :] = both.astype(BF)
+        for m in range(4):
+            both = acc[core, m] + pair_recv[k, m * 256:(m + 1) * 256, :].astype(F32)
+            rs_send[k, m * 256:(m + 1) * 256, :] = both.astype(BF)
 
         def send(j, carry):
             rs_copy(k, j).start()
@@ -185,13 +198,24 @@
         sib_copy(k).start()
 
     def out_copy(k):
-        return pltpu.make_async_copy(res_v.at[k], res_out.at[k], out_sem.at[k])
-
-    def own_copy(k):
-        return pltpu.make_async_copy(panels[k].at[z], own_out.at[k], out_sem.at[NCH + k])
+        cols = pl.ds(k * CW, CW)
+        return pltpu.make_async_copy(one_v.at[:, :, cols], one_out.at[:, :, cols], out_sem.at[k])
+
+    cp_own = pltpu.make_async_copy(own_v, own_out, out_sem.at[NCH])
 
     def stage_e(k):
         sib_copy(k).wait()
+        cols = slice(k * CW, (k + 1) * CW)
+        for m in range(4):
+            top = res_v[k, m * 256:(m + 1) * 256, :]
+            low = res_v[k, HALF + m * 256:HALF + (m + 1) * 256, :]
+            one_v[m, :256, cols] = jnp.dot(
+                inv_one_v[m, :256, :256], top, preferred_element_type=F32
+            ).astype(BF)
+            one_v[m, 256:, cols] = (
+                jnp.dot(inv_one_v[m, 256:, :256], top, preferred_element_type=F32)
+                + jnp.dot(inv_one_v[m, 256:, 256:], low, preferred_element_type=F32)
+            ).astype(BF)
         out_copy(k).start()
 
     cp_inv.wait()
@@ -199,54 +223,50 @@
     own_panel(0)
     pl.semaphore_wait(barrier, CHIPS + 2)
     z_step(0, 0)
-    for k in range(1, NCH):
-        own_panel(k)
+    own_panel(1)
+    z_step(1, 0)
+    own_panel(2)
+    own_panel(3)
+    cp_own.start()
     cp_blocks.wait()
     cp_ro.wait()
-    for k in range(NCH):
-        own_copy(k).start()
-
+    cp_inv_one.wait()
     z_step(0, 1)
     z_step(0, 2)
-    z_step(1, 0)
     z_step(0, 3)
+    z_step(1, 1)
     z_final(0)
-
-    z_step(1, 1)
     stage_a(0)
+    z_step(2, 0)
     z_step(1, 2)
     stage_b(0)
-    z_step(2, 0)
     z_step(1, 3)
+    stage_c(0)
+    z_step(2, 1)
     z_final(1)
-
-    z_step(2, 1)
     stage_a(1)
-    stage_c(0)
+    stage_d(0)
+    z_step(3, 0)
     z_step(2, 2)
     stage_b(1)
-    stage_d(0)
-    z_step(3, 0)
+    stage_e(0)
     z_step(2, 3)
+    stage_c(1)
+    z_step(3, 1)
     z_final(2)
-
-    z_step(3, 1)
-    stage_e(0)
     stage_a(2)
-    stage_c(1)
+    stage_d(1)
     z_step(3, 2)
     stage_b(2)
-    stage_d(1)
+    stage_e(1)
     z_step(3, 3)
     stage_c(2)
     z_final(3)
-
-    stage_e(1)
     stage_a(3)
+    stage_d(2)
     stage_b(3)
-    stage_d(2)
+    stage_e(2)
     stage_c(3)
-    stage_e(2)
     stage_d(3)
     stage_e(3)
 
@@ -256,15 +276,7 @@
         all_bytes(k, rs_ssem).wait()
         all_bytes(k, ag_ssem).wait()
         out_copy(k).wait()
-        own_copy(k).wait()
-
-
-def finish(inv_ref, res_ref, own_ref, one_ref, zero_ref):
-    for c in range(NCH):
-        one_ref[0, :, c * CW:(c + 1) * CW] = jnp.dot(
-            inv_ref[0], res_ref[c], preferred_element_type=F32
-        ).astype(BF)
-    zero_ref[...] = own_ref[0]
+    cp_own.wait()
 
 
 def body(
@@ -273,20 +285,23 @@
     smem = pl.BlockSpec(memory_space=pltpu.SMEM)
     hbm = pl.BlockSpec(memory_space=pl.ANY)
     dma = pltpu.SemaphoreType.DMA
-    res, own = pl.pallas_call(
+    one, zero = pl.pallas_call(
         fused,
         out_shape=(
-            jax.ShapeDtypeStruct((NCH, 4 * W, CW), BF),
-            jax.ShapeDtypeStruct((NCH, W, CW), BF),
+            jax.ShapeDtypeStruct((4, W, W), BF),
+            jax.ShapeDtypeStruct((W, W), BF),
         ),
-        in_specs=[smem, smem, smem, hbm, hbm, hbm, hbm],
+        in_specs=[smem, smem, smem, hbm, hbm, hbm, hbm, hbm],
         out_specs=(hbm, hbm),
         scratch_shapes=[
             pltpu.VMEM((W, W), BF),
             pltpu.VMEM((W, W), BF),
             pltpu.VMEM((6, W, W), BF),
             pltpu.VMEM((OWN, W), BF),
-            pltpu.VMEM((4, W, CW), F32),
+            pltpu.VMEM((4, W, W), BF),
+            pltpu.VMEM((4, W, W), BF),
+            pltpu.VMEM((W, W), BF),
+            pltpu.VMEM((2, 4, 256, CW), F32),
         ]
         + [pltpu.VMEM((NZ, W, CW), BF)] * NCH
         + [
@@ -295,39 +310,22 @@
             pltpu.VMEM((NCH, HALF, CW), BF),
             pltpu.VMEM((NCH, CHIPS - 1, OWN, CW), BF),
             pltpu.VMEM((NCH, 4 * W, CW), BF),
-            dma((4,)),
-            dma((2 * NCH,)),
+            dma((5,)),
+            dma((NCH + 1,)),
             dma((NCH,)),
-            dma((NCH, 2, 2, 4)),
+            dma((NCH, 2, 4, 4)),
             dma((NCH,)), dma((NCH,)),
             dma((NCH,)), dma((NCH,)),
             dma((NCH,)), dma((NCH,)),
             dma((NCH,)), dma((NCH,)),
         ],
         compiler_params=pltpu.CompilerParams(
-            collective_id=0, has_side_effects=True, vmem_limit_bytes=40 * 1024 * 1024
+            collective_id=0, has_side_effects=True, vmem_limit_bytes=60 * 1024 * 1024
         ),
     )(
         block_rows[0, 0], block_cols[0, 0], block_count[0],
-        inverse_zero[0, 0, 0], right_zero[0, 0, 0], factor_blocks[0, 0], right_one[0],
+        inverse_zero[0, 0, 0], right_zero[0, 0, 0], factor_blocks[0, 0], right_one[0], inverse_one[0],
     )
-    one, zero = pl.pallas_call(
-        finish,
-        grid=(4,),
-        out_shape=(
-            jax.ShapeDtypeStruct((4, W, W), BF),
-            jax.ShapeDtypeStruct((W, W), BF),
-        ),
-        in_specs=[
-            pl.BlockSpec((1, W, W), lambda m: (m, 0, 0)),
-            pl.BlockSpec((NCH, W, CW), lambda m: (0, m, 0)),
-            pl.BlockSpec((1, W, CW), lambda m: (m, 0, 0)),
-        ],
-        out_specs=(
-            pl.BlockSpec((1, W, W), lambda m: (m, 0, 0)),
-            pl.BlockSpec((W, CW), lambda m: (0, m)),
-        ),
-    )(inverse_one[0], res, own)
     return (zero[None, None, None], one[None])
 
 

time: 102 us -> 92.2 us (0.904)
  Pallas kernels: 91 us -> 85.8 us
  local copies, waits for them, and re-layouts: 9 us -> 4.91 us
    pallas_call x2 -> x1, Pallas kernels: 91 us -> 85.8 us  [body(): pl.pallas_call(fused, out_shape=(jax.ShapeDtypeStruct((4, W, W), BF), jax...]
    unnamed x16 -> x2, local copies, waits for them, and re-layouts: 9 us -> 4.91 us
where the time goes in v2:
time: 92.2 us; the launch traced here: 92 us
  Pallas kernels  85.8 us (93%)
  local copies, waits for them, and re-layouts  4.91 us (5%)
  between operations  1.29 us (1%)
    pallas_call x1, Pallas kernels, body(): pl.pallas_call(fused, out_shape=(jax.ShapeDtypeStruct((4, W, W), BF), jax...  85.8 us
    unnamed x2, local copies, waits for them, and re-layouts  4.91 us

profile of v2, /device:TPU:1, one launch (start us, length us, event | category | flops | bytes accessed | tf_op | source)
XLA Modules:
  0.0 92.0 jit_solution(10481240307136546569)
XLA Ops:
  1.3 85.8 %shard_map.95 = (bf16[4,512,512]{2,1,0:T(8,128)(2,1)}, bf16[512,512]{1,0:T(8,128)(2,1)}) custom-call(s32[6]{0:T(128)} %bitcast.18, s32[6]{0:T(128)} %bitcast.19, s32[1]{0:T(128)} %bitcast.10.count_s, bf16[512,512]{1,0:T(8,128)(2,1)} %bitcast.15, bf16[512,512]{1,0:T(8,128)(2,1)} %bitcast.16, bf16[6,512,512]{2,1,0:T(8,128)(2,1)} %bitcast.11, ...), custom_call_target="tpu_custom_call" | custom-call | tf_op jit(solution)/shard_map/pallas_call | solution.py:288
  87.1 1.9 %copy.13 = bf16[1,1,1,512,512]{4,3,2,1,0:T(8,128)(2,1)} copy(bf16[1,1,1,512,512]{4,3,2,1,0:T(8,128)(2,1)} %bitcast.17) | data formatting | bytes 1048576
  89.0 3.0 %copy.14 = bf16[1,4,512,512]{3,2,1,0:T(8,128)(2,1)} copy(bf16[1,4,512,512]{3,2,1,0:T(8,128)(2,1)} %bitcast.14) | data formatting | bytes 4194304

commit v3 on v2

--- a/solution.py
+++ b/solution.py
@@ -17,12 +17,13 @@
 CHIPS = 16
 OWN = 64
 HALF = 1024
+FAR_FIRST = (10, 6, 14, 9, 11, 2, 8, 5, 7, 13, 15, 1, 3, 4, 12)
 
 
 def fused(
-    rows_s, cols_s, count_s, inv_hbm, right_hbm, blocks_hbm, right_one_hbm, inv_one_hbm,
+    rows_hbm, cols_hbm, count_hbm, inv_hbm, right_hbm, blocks_hbm, right_one_hbm, inv_one_hbm,
     one_out, own_out,
-    inv_v, right_v, blocks_v, ro_v, inv_one_v, one_v, own_v, acc,
+    rows_s, cols_s, count_s, inv_v, right_v, blocks_v, ro_v, inv_one_v, one_v, own_v, acc,
     p0, p1, p2, p3,
     pair_send, pair_recv, rs_send, rs_recv, res_v,
     load_sem, out_sem, z_send, z_recv, pair_ssem, pair_rsem, rs_ssem, rs_rsem, ag_ssem, ag_rsem,
@@ -37,8 +38,14 @@
     down = lax.rem(z + NZ - 1, NZ)
     sibling = chip * 2 + 1 - core
 
+    cx = chip // 4
+    cy = lax.rem(chip, 4)
+
+    def chip_at(j):
+        return lax.rem(cx + j // 4, 4) * 4 + lax.rem(cy + j % 4, 4)
+
     def peer(j):
-        return lax.rem(chip + j, CHIPS) * 2 + core
+        return chip_at(j) * 2 + core
 
     cp_inv = pltpu.make_async_copy(inv_hbm, inv_v, load_sem.at[0])
     cp_right = pltpu.make_async_copy(right_hbm, right_v, load_sem.at[1])
@@ -50,11 +57,8 @@
         pl.semaphore_signal(barrier, inc=1, device_id=(r, zz), device_id_type=MESH)
     pl.semaphore_signal(barrier, inc=1, device_id=(sibling, z), device_id_type=MESH)
 
-    def greet(j, carry):
+    for j in FAR_FIRST:
         pl.semaphore_signal(barrier, inc=1, device_id=(peer(j), z), device_id_type=MESH)
-        return carry
-
-    lax.fori_loop(1, CHIPS, greet, 0)
 
     cp_blocks = pltpu.make_async_copy(blocks_hbm, blocks_v, load_sem.at[2])
     cp_blocks.start()
@@ -65,6 +69,12 @@
     cp_ro.start()
     cp_inv_one = pltpu.make_async_copy(inv_one_hbm, inv_one_v, load_sem.at[4])
     cp_inv_one.start()
+    lists = [
+        pltpu.make_async_copy(src, dst, load_sem.at[5 + i])
+        for i, (src, dst) in enumerate(((rows_hbm, rows_s), (cols_hbm, cols_s), (count_hbm, count_s)))
+    ]
+    for copy in lists:
+        copy.start()
 
     def own_panel(k):
         x = right_v[:, k * CW:(k + 1) * CW]
@@ -92,15 +102,20 @@
         piece = panels[k].at[origin, pl.ds(half * 128, 128), :]
         pltpu.make_async_copy(piece, piece, z_recv.at[k, way, half, d]).wait()
 
+    def z_pass(k, way, part, d):
+        if d > 0:
+            z_arrive(k, way, part, d - 1)
+        z_copy(k, way, part, d).start()
+
     def z_step(k, d):
+        steps = []
         for i in range(4):
             for way in range(2):
                 part = (i + 2 * way) % 4
                 far = (part < 2) if way == 0 else (part >= 2)
                 if d < 3 or far:
-                    if d > 0:
-                        z_arrive(k, way, part, d - 1)
-                    z_copy(k, way, part, d).start()
+                    steps.append(functools.partial(z_pass, k, way, part, d))
+        return steps
 
     def z_final(k):
         for part in range(4):
@@ -115,29 +130,29 @@
             device_id=(sibling, z), device_id_type=MESH,
         )
 
-    def products(k, side):
+    def product(k, side, b):
         rows = pl.ds(pl.multiple_of(side * 256, 256), 256)
-        acc[side] = jnp.zeros((4, 256, CW), F32)
-
-        def block(b, carry):
-            product = jnp.dot(blocks_v[b, rows, :], panels[k][cols_s[b]], preferred_element_type=F32)
-            used = b < count_s[0]
-            for m in range(4):
-                weight = jnp.where(jnp.logical_and(used, rows_s[b] == m), 1.0, 0.0)
-                acc[side, m] += product * weight
-            return carry
-
-        lax.fori_loop(0, 6, block, 0)
-
-    def stage_a(k):
-        products(k, 1 - core)
+        value = jnp.dot(blocks_v[b, rows, :], panels[k][cols_s[b]], preferred_element_type=F32)
+        used = b < count_s[0]
+        for m in range(4):
+            weight = jnp.where(jnp.logical_and(used, rows_s[b] == m), 1.0, 0.0)
+            if b == 0:
+                acc[side, m] = value * weight
+            else:
+                acc[side, m] += value * weight
+
+    def send_away(k):
         for m in range(4):
             pair_send[k, m * 256:(m + 1) * 256, :] = acc[1 - core, m].astype(BF)
         pair_copy(k).start()
-        products(k, core)
+
+    def stage_a(k):
+        away = [functools.partial(product, k, 1 - core, b) for b in range(6)]
+        keep = [functools.partial(product, k, core, b) for b in range(6)]
+        return away + [functools.partial(send_away, k)] + keep
 
     def rs_copy(k, j):
-        target = lax.rem(chip + j, CHIPS)
+        target = chip_at(j)
         return pltpu.make_async_remote_copy(
             src_ref=rs_send.at[k, pl.ds(pl.multiple_of(target * OWN, OWN), OWN), :],
             dst_ref=rs_recv.at[k, j - 1],
@@ -151,11 +166,8 @@
             both = acc[core, m] + pair_recv[k, m * 256:(m + 1) * 256, :].astype(F32)
             rs_send[k, m * 256:(m + 1) * 256, :] = both.astype(BF)
 
-        def send(j, carry):
+        for j in FAR_FIRST:
             rs_copy(k, j).start()
-            return carry
-
-        lax.fori_loop(1, CHIPS, send, 0)
 
     def own_rows():
         return pl.ds(pl.multiple_of(core * HALF + chip * OWN, OWN), OWN)
@@ -179,11 +191,8 @@
         left = ro_v[:, k * CW:(k + 1) * CW].astype(F32) - total
         res_v[k, own_rows(), :] = left.astype(BF)
 
-        def send(j, carry):
+        for j in FAR_FIRST:
             ag_copy(k, j).start()
-            return carry
-
-        lax.fori_loop(1, CHIPS, send, 0)
 
     def sib_copy(k):
         piece = res_v.at[k, pl.ds(pl.multiple_of(core * HALF, HALF), HALF), :]
@@ -222,53 +231,65 @@
     cp_right.wait()
     own_panel(0)
     pl.semaphore_wait(barrier, CHIPS + 2)
-    z_step(0, 0)
-    own_panel(1)
-    z_step(1, 0)
-    own_panel(2)
-    own_panel(3)
-    cp_own.start()
-    cp_blocks.wait()
-    cp_ro.wait()
-    cp_inv_one.wait()
-    z_step(0, 1)
-    z_step(0, 2)
-    z_step(0, 3)
-    z_step(1, 1)
-    z_final(0)
-    stage_a(0)
-    z_step(2, 0)
-    z_step(1, 2)
-    stage_b(0)
-    z_step(1, 3)
-    stage_c(0)
-    z_step(2, 1)
-    z_final(1)
-    stage_a(1)
-    stage_d(0)
-    z_step(3, 0)
-    z_step(2, 2)
-    stage_b(1)
-    stage_e(0)
-    z_step(2, 3)
-    stage_c(1)
-    z_step(3, 1)
-    z_final(2)
-    stage_a(2)
-    stage_d(1)
-    z_step(3, 2)
-    stage_b(2)
-    stage_e(1)
-    z_step(3, 3)
-    stage_c(2)
-    z_final(3)
-    stage_a(3)
-    stage_d(2)
-    stage_b(3)
-    stage_e(2)
-    stage_c(3)
-    stage_d(3)
-    stage_e(3)
+    def loaded():
+        cp_own.start()
+        cp_blocks.wait()
+        for copy in lists:
+            copy.wait()
+        cp_ro.wait()
+        cp_inv_one.wait()
+
+    schedule = (
+        (z_step(0, 0),),
+        ([functools.partial(own_panel, 1)],),
+        (z_step(1, 0),),
+        ([functools.partial(own_panel, 2)],),
+        ([functools.partial(own_panel, 3)],),
+        ([loaded],),
+        (z_step(0, 1),),
+        (z_step(1, 1),),
+        (z_step(0, 2),),
+        (z_step(0, 3),),
+        (z_step(2, 0),),
+        (z_step(1, 2),),
+        ([functools.partial(z_final, 0)],),
+        (stage_a(0),),
+        (z_step(2, 1),),
+        ([functools.partial(stage_b, 0)],),
+        (z_step(1, 3),),
+        (z_step(2, 2),),
+        (z_step(3, 0),),
+        ([functools.partial(z_final, 1)],),
+        (stage_a(1),),
+        (z_step(2, 3),),
+        ([functools.partial(stage_c, 0)],),
+        ([functools.partial(stage_b, 1)],),
+        (z_step(3, 1),),
+        ([functools.partial(z_final, 2)],),
+        (stage_a(2), z_step(3, 2),),
+        ([functools.partial(stage_d, 0)],),
+        ([functools.partial(stage_b, 2)],),
+        ([functools.partial(stage_c, 1)],),
+        (z_step(3, 3),),
+        ([functools.partial(stage_e, 0)],),
+        ([functools.partial(stage_d, 1)],),
+        ([functools.partial(z_final, 3)],),
+        (stage_a(3),),
+        ([functools.partial(stage_b, 3)],),
+        ([functools.partial(stage_c, 2)],),
+        ([functools.partial(stage_e, 1)],),
+        ([functools.partial(stage_c, 3)],),
+        ([functools.partial(stage_d, 2)],),
+        ([functools.partial(stage_e, 2)],),
+        ([functools.partial(stage_d, 3)],),
+        ([functools.partial(stage_e, 3)],),
+    )
+    for phase in schedule:
+        longest = max(len(steps) for steps in phase)
+        for i in range(longest):
+            for steps in phase:
+                for step in steps[i * len(steps) // longest:(i + 1) * len(steps) // longest]:
+                    step()
 
     for k in range(NCH):
         piece = panels[k].at[0:7]
@@ -282,7 +303,6 @@
 def body(
     right_zero, inverse_zero, factor_blocks, block_rows, block_cols, block_count, right_one, inverse_one,
 ):
-    smem = pl.BlockSpec(memory_space=pltpu.SMEM)
     hbm = pl.BlockSpec(memory_space=pl.ANY)
     dma = pltpu.SemaphoreType.DMA
     one, zero = pl.pallas_call(
@@ -291,9 +311,12 @@
             jax.ShapeDtypeStruct((4, W, W), BF),
             jax.ShapeDtypeStruct((W, W), BF),
         ),
-        in_specs=[smem, smem, smem, hbm, hbm, hbm, hbm, hbm],
+        in_specs=[hbm, hbm, hbm, hbm, hbm, hbm, hbm, hbm],
         out_specs=(hbm, hbm),
         scratch_shapes=[
+            pltpu.SMEM((6,), jnp.int32),
+            pltpu.SMEM((6,), jnp.int32),
+            pltpu.SMEM((1,), jnp.int32),
             pltpu.VMEM((W, W), BF),
             pltpu.VMEM((W, W), BF),
             pltpu.VMEM((6, W, W), BF),
@@ -310,7 +333,7 @@
             pltpu.VMEM((NCH, HALF, CW), BF),
             pltpu.VMEM((NCH, CHIPS - 1, OWN, CW), BF),
             pltpu.VMEM((NCH, 4 * W, CW), BF),
-            dma((5,)),
+            dma((8,)),
             dma((NCH + 1,)),
             dma((NCH,)),
             dma((NCH, 2, 4, 4)),
@@ -320,11 +343,17 @@
             dma((NCH,)), dma((NCH,)),
         ],
         compiler_params=pltpu.CompilerParams(
-            collective_id=0, has_side_effects=True, vmem_limit_bytes=60 * 1024 * 1024
+            collective_id=0, has_side_effects=True, vmem_limit_bytes=40 * 1024 * 1024
         ),
     )(
         block_rows[0, 0], block_cols[0, 0], block_count[0],
-        inverse_zero[0, 0, 0], right_zero[0, 0, 0], factor_blocks[0, 0], right_one[0], inverse_one[0],
+        *(
+            pltpu.with_memory_space_constraint(operand, pltpu.HBM)
+            for operand in (
+                inverse_zero[0, 0, 0], right_zero[0, 0, 0],
+                factor_blocks[0, 0], right_one[0], inverse_one[0],
+            )
+        ),
     )
     return (zero[None, None, None], one[None])
 

time: 92.2 us -> 80.2 us (0.87)
  Pallas kernels: 85.8 us -> 75.3 us
  local copies, waits for them, and re-layouts: 4.91 us -> 3.42 us
    pallas_call x1, Pallas kernels: 85.8 us -> 75.3 us  [body(): pl.pallas_call(fused, out_shape=(jax.ShapeDtypeStruct((4, W, W), BF), jax...]
    unnamed x2 -> x6, local copies, waits for them, and re-layouts: 4.91 us -> 3.42 us
where the time goes in v3:
time: 80.2 us; the launch traced here: 80 us
  Pallas kernels  75.3 us (94%)
  local copies, waits for them, and re-layouts  3.42 us (4%)
  between operations  1.3 us (2%)
    pallas_call x1, Pallas kernels, body(): pl.pallas_call(fused, out_shape=(jax.ShapeDtypeStruct((4, W, W), BF), jax...  75.3 us
    unnamed x6, local copies, waits for them, and re-layouts  3.42 us

profile of v3, /device:TPU:1, one launch (start us, length us, event | category | flops | bytes accessed | tf_op | source)
XLA Modules:
  0.0 80.0 jit_solution(16702546578532353165)
XLA Ops:
  1.3 0.0 copy-start
  1.3 0.6 copy-done
  1.9 0.0 copy-start.1
  1.9 0.7 copy-done.1
  2.6 75.3 %shard_map.95 = (bf16[4,512,512]{2,1,0:T(8,128)(2,1)S(1)}, bf16[512,512]{1,0:T(8,128)(2,1)S(1)}) custom-call(s32[6]{0:T(128)S(1)} %bitcast.13, s32[6]{0:T(128)S(1)} %bitcast.14, s32[1]{0:T(128)} %bitcast.10.count_hbm, bf16[512,512]{1,0:T(8,128)(2,1)} %bitcast.18, bf16[512,512]{1,0:T(8,128)(2,1)} %bitcast.19, bf16[6,512,512]{2,1,0:T(8,128)(2,1)} %bitcast.15, ...), custom_call_target="tpu_custom_call" | custom-call | tf_op jit(solution)/shard_map/pallas_call | solution.py:308
  77.9 0.8 copy.13
  78.7 1.3 %copy.14 = bf16[1,4,512,512]{3,2,1,0:T(8,128)(2,1)} copy(bf16[1,4,512,512]{3,2,1,0:T(8,128)(2,1)S(1)} %bitcast.11) | data formatting | bytes 4194304
Async XLA Ops:
  1.3 0.7 copy-start
  1.9 0.7 copy-start.1

commit v4 on v3

--- a/solution.py
+++ b/solution.py
@@ -22,11 +22,11 @@
 
 def fused(
     rows_hbm, cols_hbm, count_hbm, inv_hbm, right_hbm, blocks_hbm, right_one_hbm, inv_one_hbm,
-    one_out, own_out,
-    rows_s, cols_s, count_s, inv_v, right_v, blocks_v, ro_v, inv_one_v, one_v, own_v, acc,
+    one_v, own_v,
+    rows_s, cols_s, count_s, inv_v, right_v, blocks_v, ro_v, inv_one_v, acc,
     p0, p1, p2, p3,
     pair_send, pair_recv, rs_send, rs_recv, res_v,
-    load_sem, out_sem, z_send, z_recv, pair_ssem, pair_rsem, rs_ssem, rs_rsem, ag_ssem, ag_rsem,
+    load_sem, z_send, z_recv, pair_ssem, pair_rsem, rs_ssem, rs_rsem, ag_ssem, ag_rsem,
     sib_ssem, sib_rsem,
 ):
     panels = (p0, p1, p2, p3)
@@ -206,12 +206,6 @@
         all_bytes(k, ag_rsem).wait()
         sib_copy(k).start()
 
-    def out_copy(k):
-        cols = pl.ds(k * CW, CW)
-        return pltpu.make_async_copy(one_v.at[:, :, cols], one_out.at[:, :, cols], out_sem.at[k])
-
-    cp_own = pltpu.make_async_copy(own_v, own_out, out_sem.at[NCH])
-
     def stage_e(k):
         sib_copy(k).wait()
         cols = slice(k * CW, (k + 1) * CW)
@@ -225,14 +219,12 @@
                 jnp.dot(inv_one_v[m, 256:, :256], top, preferred_element_type=F32)
                 + jnp.dot(inv_one_v[m, 256:, 256:], low, preferred_element_type=F32)
             ).astype(BF)
-        out_copy(k).start()
 
     cp_inv.wait()
     cp_right.wait()
     own_panel(0)
     pl.semaphore_wait(barrier, CHIPS + 2)
     def loaded():
-        cp_own.start()
         cp_blocks.wait()
         for copy in lists:
             copy.wait()
@@ -296,14 +288,13 @@
         pltpu.make_async_copy(piece, piece, z_send.at[k]).wait()
         all_bytes(k, rs_ssem).wait()
         all_bytes(k, ag_ssem).wait()
-        out_copy(k).wait()
-    cp_own.wait()
 
 
 def body(
     right_zero, inverse_zero, factor_blocks, block_rows, block_cols, block_count, right_one, inverse_one,
 ):
     hbm = pl.BlockSpec(memory_space=pl.ANY)
+    vm = pl.BlockSpec(memory_space=pltpu.VMEM)
     dma = pltpu.SemaphoreType.DMA
     one, zero = pl.pallas_call(
         fused,
@@ -312,7 +303,7 @@
             jax.ShapeDtypeStruct((W, W), BF),
         ),
         in_specs=[hbm, hbm, hbm, hbm, hbm, hbm, hbm, hbm],
-        out_specs=(hbm, hbm),
+        out_specs=(vm, vm),
         scratch_shapes=[
             pltpu.SMEM((6,), jnp.int32),
             pltpu.SMEM((6,), jnp.int32),
@@ -322,8 +313,6 @@
             pltpu.VMEM((6, W, W), BF),
             pltpu.VMEM((OWN, W), BF),
             pltpu.VMEM((4, W, W), BF),
-            pltpu.VMEM((4, W, W), BF),
-            pltpu.VMEM((W, W), BF),
             pltpu.VMEM((2, 4, 256, CW), F32),
         ]
         + [pltpu.VMEM((NZ, W, CW), BF)] * NCH
@@ -334,7 +323,6 @@
             pltpu.VMEM((NCH, CHIPS - 1, OWN, CW), BF),
             pltpu.VMEM((NCH, 4 * W, CW), BF),
             dma((8,)),
-            dma((NCH + 1,)),
             dma((NCH,)),
             dma((NCH, 2, 4, 4)),
             dma((NCH,)), dma((NCH,)),
@@ -346,7 +334,9 @@
             collective_id=0, has_side_effects=True, vmem_limit_bytes=40 * 1024 * 1024
         ),
     )(
-        block_rows[0, 0], block_cols[0, 0], block_count[0],
+        pltpu.with_memory_space_constraint(block_rows[0, 0], pltpu.HBM),
+        pltpu.with_memory_space_constraint(block_cols[0, 0], pltpu.HBM),
+        block_count[0],
         *(
             pltpu.with_memory_space_constraint(operand, pltpu.HBM)
             for operand in (

time: 80.2 us -> 78.8 us (0.983)
  local copies, waits for them, and re-layouts: 3.42 us -> 2.11 us
    unnamed x6 -> x2, local copies, waits for them, and re-layouts: 3.42 us -> 2.11 us
where the time goes in v4:
time: 78.8 us; the launch traced here: 78.7 us
  Pallas kernels  75.3 us (96%)
  local copies, waits for them, and re-layouts  2.11 us (3%)
  between operations  1.29 us (2%)
    pallas_call x1, Pallas kernels, body(): pl.pallas_call(fused, out_shape=(jax.ShapeDtypeStruct((4, W, W), BF), jax...  75.3 us
    unnamed x2, local copies, waits for them, and re-layouts  2.11 us

profile of v4, /device:TPU:1, one launch (start us, length us, event | category | flops | bytes accessed | tf_op | source)
XLA Modules:
  0.0 78.7 jit_solution(16449676669553133505)
XLA Ops:
  1.3 75.3 %shard_map.95 = (bf16[4,512,512]{2,1,0:T(8,128)(2,1)S(1)}, bf16[512,512]{1,0:T(8,128)(2,1)S(1)}) custom-call(s32[6]{0:T(128)} %bitcast.18, s32[6]{0:T(128)} %bitcast.19, s32[1]{0:T(128)} %bitcast.10.count_hbm, bf16[512,512]{1,0:T(8,128)(2,1)} %bitcast.16, bf16[512,512]{1,0:T(8,128)(2,1)} %bitcast.17, bf16[6,512,512]{2,1,0:T(8,128)(2,1)} %bitcast.13, ...), custom_call_target="tpu_custom_call" | custom-call | tf_op jit(solution)/shard_map/pallas_call | solution.py:299
  76.6 0.8 %copy.13 = bf16[1,1,1,512,512]{4,3,2,1,0:T(8,128)(2,1)} copy(bf16[1,1,1,512,512]{4,3,2,1,0:T(8,128)(2,1)S(1)} %bitcast.12) | data formatting | bytes 1048576
  77.4 1.3 %copy.14 = bf16[1,4,512,512]{3,2,1,0:T(8,128)(2,1)} copy(bf16[1,4,512,512]{3,2,1,0:T(8,128)(2,1)S(1)} %bitcast.11) | data formatting | bytes 4194304

commit v5 on v4

--- a/solution.py
+++ b/solution.py
@@ -259,18 +259,18 @@
         (z_step(3, 1),),
         ([functools.partial(z_final, 2)],),
         (stage_a(2), z_step(3, 2),),
+        ([functools.partial(stage_b, 2)],),
         ([functools.partial(stage_d, 0)],),
-        ([functools.partial(stage_b, 2)],),
+        (z_step(3, 3),),
         ([functools.partial(stage_c, 1)],),
-        (z_step(3, 3),),
         ([functools.partial(stage_e, 0)],),
-        ([functools.partial(stage_d, 1)],),
         ([functools.partial(z_final, 3)],),
         (stage_a(3),),
         ([functools.partial(stage_b, 3)],),
         ([functools.partial(stage_c, 2)],),
+        ([functools.partial(stage_d, 1)],),
+        ([functools.partial(stage_c, 3)],),
         ([functools.partial(stage_e, 1)],),
-        ([functools.partial(stage_c, 3)],),
         ([functools.partial(stage_d, 2)],),
         ([functools.partial(stage_e, 2)],),
         ([functools.partial(stage_d, 3)],),

time: 78.8 us -> 75 us (0.952)
  Pallas kernels: 75.3 us -> 71.5 us
    pallas_call x1, Pallas kernels: 75.3 us -> 71.5 us  [body(): pl.pallas_call(fused, out_shape=(jax.ShapeDtypeStruct((4, W, W), BF), jax...]
where the time goes in v5:
time: 75 us; the launch traced here: 74.9 us
  Pallas kernels  71.5 us (95%)
  local copies, waits for them, and re-layouts  2.11 us (3%)
  between operations  1.29 us (2%)
    pallas_call x1, Pallas kernels, body(): pl.pallas_call(fused, out_shape=(jax.ShapeDtypeStruct((4, W, W), BF), jax...  71.5 us
    unnamed x2, local copies, waits for them, and re-layouts  2.11 us

profile of v5, /device:TPU:1, one launch (start us, length us, event | category | flops | bytes accessed | tf_op | source)
XLA Modules:
  0.0 74.9 jit_solution(7108140643974150030)
XLA Ops:
  1.3 71.5 %shard_map.95 = (bf16[4,512,512]{2,1,0:T(8,128)(2,1)S(1)}, bf16[512,512]{1,0:T(8,128)(2,1)S(1)}) custom-call(s32[6]{0:T(128)} %bitcast.18, s32[6]{0:T(128)} %bitcast.19, s32[1]{0:T(128)} %bitcast.10.count_hbm, bf16[512,512]{1,0:T(8,128)(2,1)} %bitcast.16, bf16[512,512]{1,0:T(8,128)(2,1)} %bitcast.17, bf16[6,512,512]{2,1,0:T(8,128)(2,1)} %bitcast.13, ...), custom_call_target="tpu_custom_call" | custom-call | tf_op jit(solution)/shard_map/pallas_call | solution.py:299
  72.7 0.8 %copy.13 = bf16[1,1,1,512,512]{4,3,2,1,0:T(8,128)(2,1)} copy(bf16[1,1,1,512,512]{4,3,2,1,0:T(8,128)(2,1)S(1)} %bitcast.12) | data formatting | bytes 1048576
  73.5 1.3 %copy.14 = bf16[1,4,512,512]{3,2,1,0:T(8,128)(2,1)} copy(bf16[1,4,512,512]{3,2,1,0:T(8,128)(2,1)S(1)} %bitcast.11) | data formatting | bytes 4194304
